TPU v7x, 32 devices: a whole 2x2x4 slice. The times are simulated.
32 devices in a mesh: rep: 4 (over x, core), shard: 8 (over z, y).
Axes of the slice: x: 2, y: 2, z: 4, core: 2. Of those that a mesh axis runs over, the one named last changes fastest.
Arguments:
- tokens: bfloat16 [4096, 896], P(('rep', 'shard')), may hold values from -6 to 6
- cotangent: bfloat16 [4096, 896], P(('rep', 'shard')), may hold values from -6 to 6
- lengths: int32 [32, 8], P(('rep', 'shard')), may hold values from 1 to 64, 128 in all within a row
- query_weight: bfloat16 [896, 896], P('shard'), may hold values from -0.1875 to 0.1875
- key_weight: bfloat16 [896, 128], P('shard'), may hold values from -0.1875 to 0.1875
- value_weight: bfloat16 [896, 128], P('shard'), may hold values from -0.1875 to 0.1875
- output_weight: bfloat16 [896, 896], P('shard'), may hold values from -0.5 to 0.5
- query_bias: bfloat16 [896], P('shard'), may hold values from -3 to 3
- key_bias: bfloat16 [128], P('shard'), may hold values from -3 to 3
- value_bias: bfloat16 [128], P('shard'), may hold values from -3 to 3
- attn_gain: bfloat16 [896], P('shard'), may hold values from 0.5 to 1.5
- gate_weight: bfloat16 [896, 4864], P('shard'), may hold values from -0.1875 to 0.1875
- up_weight: bfloat16 [896, 4864], P('shard'), may hold values from -0.1875 to 0.1875
- down_weight: bfloat16 [4864, 896], P('shard'), may hold values from -0.15625 to 0.15625
- mlp_gain: bfloat16 [896], P('shard'), may hold values from 0.5 to 1.5
Outputs:
- result: bfloat16 [4096, 896], P(('rep', 'shard'))
- grad_tokens: float32 [4096, 896], P(('rep', 'shard'))
- grad_query_weight: float32 [896, 896], P('shard')
- grad_key_weight: float32 [896, 128], P('shard')
- grad_value_weight: float32 [896, 128], P('shard')
- grad_output_weight: float32 [896, 896], P('shard')
- grad_query_bias: float32 [896], P('shard')
- grad_key_bias: float32 [128], P('shard')
- grad_value_bias: float32 [128], P('shard')
- grad_attn_gain: float32 [896], P('shard')
- grad_gate_weight: float32 [896, 4864], P('shard')
- grad_up_weight: float32 [896, 4864], P('shard')
- grad_down_weight: float32 [4864, 896], P('shard')
- grad_mlp_gain: float32 [896], P('shard')
Inputs may be any that keep to these rules, and one draw needn't show every extreme that they name: Row b lists the lengths of the 8 sequences packed in order on the b-th block of 128 tokens; they fill it exactly, and the longest of every row is exactly 64.
All inputs are finite; a program needn't handle non-finite values.
Results may differ from a plain program's by a relative error of at most 0.02.
The roundings to bfloat16 on the way count: a program that leaves them out, or rounds other values in their place, can miss the bound.
Values may be sent and summed in bfloat16 or wider, within the bound.
A program may use at most 192 MiB of HBM per device.

v0:
```python
import math
import jax
import jax.numpy as jnp
from jax import lax
from jax.sharding import PartitionSpec as P

HEADS = 14
KVH = 2
HD = 64
theta_base = 1000000.0
eps_norm = 1e-06
masked_score = -1000000000.0


def times_transposed(left, weight):
    return lax.dot_general(
        left, weight, (((1,), (1,)), ((), ())), preferred_element_type=jnp.float32
    )


def tables(lengths_row, rows):
    ends = jnp.cumsum(lengths_row)
    starts = ends - lengths_row
    places = jnp.arange(rows, dtype=jnp.int32)
    inside = ((places[:, None] >= starts[None, :]) & (places[:, None] < ends[None, :])).astype(
        jnp.int32
    )
    slots = jnp.arange(lengths_row.shape[0], dtype=jnp.int32)
    segment = jnp.sum(inside * slots[None, :], axis=1)
    first = jnp.sum(inside * starts[None, :], axis=1)
    offset = (places - first).astype(jnp.float32)
    half = HD // 2
    freq = theta_base ** (-(jnp.arange(half, dtype=jnp.float32) * (2.0 / HD)))
    angles = offset[:, None] * freq[None, :]
    return (segment, places, jnp.cos(angles), jnp.sin(angles))


def rotate(values, cosine, sine):
    half = values.shape[-1] // 2
    first, second = (values[..., :half], values[..., half:])
    cosine = cosine[:, :, None, :]
    sine = sine[:, :, None, :]
    return jnp.concatenate(
        [first * cosine - second * sine, second * cosine + first * sine], axis=-1
    )


def unrotate(grads, cosine, sine):
    half = grads.shape[-1] // 2
    first, second = (grads[..., :half], grads[..., half:])
    cosine = cosine[:, :, None, :]
    sine = sine[:, :, None, :]
    return jnp.concatenate(
        [first * cosine + second * sine, second * cosine - first * sine], axis=-1
    )


def norm_fwd(hidden, gain):
    scale = lax.rsqrt(jnp.mean(hidden * hidden, axis=-1, keepdims=True) + eps_norm)
    return (scale, hidden * scale * gain.astype(jnp.float32))


def norm_bwd(dnormed, hidden, scale, gain):
    gain_f = gain.astype(jnp.float32)
    dgain = jnp.sum(dnormed * hidden * scale, axis=0)
    inner = dnormed * gain_f
    dhidden = scale * inner - hidden * (scale * scale * scale) * jnp.mean(
        inner * hidden, axis=-1, keepdims=True
    )
    return (dhidden, dgain)


def scores_of(query, keys, segment, places):
    raw = jnp.einsum("igha,jga->ghij", query, keys, preferred_element_type=jnp.float32) * (
        1.0 / math.sqrt(HD)
    )
    allowed = (segment[:, None] == segment[None, :]) & (places[None, :] <= places[:, None])
    return jnp.where(allowed[None, None], raw, masked_score)


def attend(query, keys, values, segment, places):
    raw = scores_of(query, keys, segment, places)
    top = jnp.max(raw, axis=-1, keepdims=True)
    total = jnp.sum(jnp.exp(raw - top), axis=-1)
    lse = top[..., 0] + jnp.log(total)
    probs = jnp.exp(raw - lse[..., None]).astype(jnp.bfloat16)
    mixed = jnp.einsum("ghij,jga->igha", probs, values, preferred_element_type=jnp.float32).astype(
        jnp.bfloat16
    )
    return (mixed, lse)


def attend_back(query, keys, values, mixed, dmixed, lse, segment, places):
    raw = scores_of(query, keys, segment, places)
    probs_f = jnp.exp(raw - lse[..., None])
    probs = probs_f.astype(jnp.bfloat16)
    dvals = jnp.einsum("ghij,igha->jga", probs, dmixed, preferred_element_type=jnp.float32)
    dprobs = jnp.einsum("igha,jga->ghij", dmixed, values, preferred_element_type=jnp.float32)
    delta = jnp.einsum("igha,igha->ghi", dmixed, mixed, preferred_element_type=jnp.float32)
    dscores = (probs_f * (dprobs - delta[..., None]) * (1.0 / math.sqrt(HD))).astype(jnp.bfloat16)
    dquery = jnp.einsum("ghij,jga->igha", dscores, keys, preferred_element_type=jnp.float32)
    dkeys = jnp.einsum("ghij,igha->jga", dscores, query, preferred_element_type=jnp.float32)
    return (dquery, dkeys, dvals)


def pad_rows(vector, rows):
    return jnp.pad(vector, (0, rows - vector.shape[0]))


def share_of(weight, index, shards, shares):
    width = weight.shape[1] // shards
    part = width // shares
    return jnp.concatenate(
        [
            lax.dynamic_slice(weight, (0, s * width + index * part), (weight.shape[0], part))
            for s in range(shards)
        ],
        axis=1,
    )


def on_device(
    tokens,
    cotangent,
    lengths,
    query_weight,
    key_weight,
    value_weight,
    output_weight,
    query_bias,
    key_bias,
    value_bias,
    attn_gain,
    gate_weight,
    up_weight,
    down_weight,
    mlp_gain,
):
    shards = lax.axis_size("shard")
    reps = lax.axis_size("rep")
    rep = lax.axis_index("rep")
    rows, width = tokens.shape
    own = query_weight.shape[0]
    kvd = key_weight.shape[1]
    own_kv = key_bias.shape[0]
    small_w = 128
    f32, bf16 = (jnp.float32, jnp.bfloat16)
    small = jnp.stack(
        [query_bias, attn_gain, mlp_gain, pad_rows(key_bias, own), pad_rows(value_bias, own)],
        axis=1,
    )
    small = jnp.pad(small, ((0, 0), (0, small_w - small.shape[1])))
    packed = jnp.concatenate([query_weight, key_weight, value_weight, output_weight, small], axis=1)
    packed = lax.all_gather(packed, "shard", axis=0, tiled=True)
    wide = width + 2 * kvd
    qkv_weight = packed[:, :wide]
    output_full = packed[:, wide : wide + width]
    vectors = packed[:, wide + width : wide + width + 5].T
    query_bias_f, attn_gain_f, mlp_gain_f = (vectors[0], vectors[1], vectors[2])
    key_bias_f = vectors[3].reshape(shards, own)[:, :own_kv].reshape(kvd)
    value_bias_f = vectors[4].reshape(shards, own)[:, :own_kv].reshape(kvd)
    qkv_bias = jnp.concatenate([query_bias_f, key_bias_f, value_bias_f]).astype(f32)
    part = down_weight.shape[0] // reps
    gate_mine = lax.all_gather(
        share_of(gate_weight, rep, shards, reps), "shard", axis=0, tiled=True
    )
    up_mine = lax.all_gather(share_of(up_weight, rep, shards, reps), "shard", axis=0, tiled=True)
    down_mine = lax.all_gather(
        lax.dynamic_slice(down_weight, (rep * part, 0), (part, width)), "shard", axis=0, tiled=True
    )
    cot_all = lax.all_gather(cotangent, "rep", axis=0, tiled=True)
    segment, places, cosine, sine = jax.vmap(lambda lens: tables(lens, rows))(lengths)
    flat = tokens.astype(f32)
    scale_one, normed_one = norm_fwd(flat, attn_gain_f)
    normed_one = normed_one.astype(bf16)
    qkv = jnp.dot(normed_one, qkv_weight, preferred_element_type=f32) + qkv_bias
    query = rotate(qkv[:, :width].reshape(1, rows, HEADS, HD), cosine, sine).astype(bf16)
    query = query.reshape(1, rows, KVH, HEADS // KVH, HD)
    keys = rotate(qkv[:, width : width + kvd].reshape(1, rows, KVH, HD), cosine, sine).astype(bf16)
    values = qkv[:, width + kvd :].reshape(1, rows, KVH, HD).astype(bf16)
    mixed, lse = jax.vmap(attend)(query, keys, values, segment, places)
    mixed_flat = mixed.reshape(rows, width)
    hidden_one = flat + jnp.dot(mixed_flat, output_full, preferred_element_type=f32)
    scale_two, normed_two = norm_fwd(hidden_one, mlp_gain_f)
    normed_all = lax.all_gather(normed_two.astype(bf16), "rep", axis=0, tiled=True)
    gate = jnp.dot(normed_all, gate_mine, preferred_element_type=f32)
    upper = jnp.dot(normed_all, up_mine, preferred_element_type=f32)
    sigma = jax.nn.sigmoid(gate)
    product = (gate * sigma * upper).astype(bf16)
    dprod = times_transposed(cot_all, down_mine)
    dgate = (dprod * upper * sigma * (1.0 + gate * (1.0 - sigma))).astype(bf16)
    dup = (dprod * gate * sigma).astype(bf16)
    dnormed_part = times_transposed(dgate, gate_mine) + times_transposed(dup, up_mine)
    dnormed_two = lax.psum_scatter(
        dnormed_part.astype(bf16), "rep", scatter_dimension=0, tiled=True
    ).astype(f32)
    grad_down = jnp.dot(product.T, cot_all, preferred_element_type=f32).astype(bf16)
    grad_gate = jnp.dot(normed_all.T, dgate, preferred_element_type=f32).astype(bf16)
    grad_up = jnp.dot(normed_all.T, dup, preferred_element_type=f32).astype(bf16)
    down_owned = lax.psum_scatter(grad_down, "shard", scatter_dimension=0, tiled=True)
    gate_owned = lax.psum_scatter(grad_gate, "shard", scatter_dimension=0, tiled=True)
    up_owned = lax.psum_scatter(grad_up, "shard", scatter_dimension=0, tiled=True)
    out_part = jnp.dot(product, down_mine, preferred_element_type=f32).astype(bf16)
    out_sum = lax.psum_scatter(out_part, "rep", scatter_dimension=0, tiled=True)
    result = (hidden_one + out_sum.astype(f32)).astype(bf16)
    dh_two, grad_mlp_gain = norm_bwd(dnormed_two, hidden_one, scale_two, mlp_gain_f)
    dhidden = cotangent.astype(f32) + dh_two
    dres = dhidden.astype(bf16)
    grad_output = jnp.dot(mixed_flat.T, dres, preferred_element_type=f32).astype(bf16)
    dmixed = times_transposed(dres, output_full).astype(bf16)
    dmixed = dmixed.reshape(1, rows, KVH, HEADS // KVH, HD)
    dquery, dkeys, dvals = jax.vmap(attend_back)(
        query, keys, values, mixed, dmixed, lse, segment, places
    )
    dquery = unrotate(dquery.reshape(1, rows, HEADS, HD), cosine, sine).reshape(rows, width)
    dkeys = unrotate(dkeys, cosine, sine).reshape(rows, kvd)
    dvals = dvals.reshape(rows, kvd)
    dqkv = jnp.concatenate([dquery, dkeys, dvals], axis=1)
    grad_bias = jnp.sum(dqkv, axis=0)
    dqkv_b = dqkv.astype(bf16)
    grad_qkv = jnp.dot(normed_one.T, dqkv_b, preferred_element_type=f32).astype(bf16)
    dnormed_one = times_transposed(dqkv_b, qkv_weight)
    dh_one, grad_attn_gain = norm_bwd(dnormed_one, flat, scale_one, attn_gain_f)
    grad_input = dhidden + dh_one
    spread = lambda v: jnp.pad(v.reshape(shards, own_kv), ((0, 0), (0, own - own_kv))).reshape(
        width
    )
    small_g = jnp.stack(
        [
            grad_bias[:width],
            grad_attn_gain,
            grad_mlp_gain,
            spread(grad_bias[width : width + kvd]),
            spread(grad_bias[width + kvd :]),
        ],
        axis=0,
    )
    small_g = jnp.pad(small_g, ((0, small_w - small_g.shape[0]), (0, 0))).T.astype(bf16)
    packed_g = jnp.concatenate([grad_qkv, grad_output, small_g], axis=1)
    owned = lax.psum_scatter(packed_g, "shard", scatter_dimension=0, tiled=True)
    total_w = wide + width
    share_w = total_w // reps
    chunks = [
        jnp.concatenate([owned[:, i * share_w : (i + 1) * share_w], owned[:, total_w:]], axis=1)
        for i in range(reps)
    ]
    split = lax.psum_scatter(
        jnp.concatenate(chunks, axis=0), "rep", scatter_dimension=0, tiled=True
    )
    vec = split[:, share_w : share_w + 5].astype(f32).T
    attn_all = lax.all_gather(split[:, :share_w], "rep", axis=0)
    attn_all = jnp.concatenate([attn_all[i] for i in range(reps)], axis=1).astype(f32)
    down_all = lax.all_gather(down_owned, "rep", axis=0, tiled=True).astype(f32)

    def joined(share):
        every = lax.all_gather(share, "rep", axis=0)
        return jnp.concatenate(
            [every[r][:, s * part : (s + 1) * part] for s in range(shards) for r in range(reps)],
            axis=1,
        ).astype(f32)

    return (
        result,
        grad_input,
        attn_all[:, :width],
        attn_all[:, width : width + kvd],
        attn_all[:, width + kvd : wide],
        attn_all[:, wide:],
        vec[0],
        vec[3][:own_kv],
        vec[4][:own_kv],
        vec[1],
        joined(gate_owned),
        joined(up_owned),
        down_all,
        vec[2],
    )


def solution(mesh):
    in_specs = (
        P(("rep", "shard"), None),
        P(("rep", "shard"), None),
        P(("rep", "shard"), None),
        P("shard", None),
        P("shard", None),
        P("shard", None),
        P("shard", None),
        P("shard"),
        P("shard"),
        P("shard"),
        P("shard"),
        P("shard", None),
        P("shard", None),
        P("shard", None),
        P("shard"),
    )
    out_specs = (
        P(("rep", "shard"), None),
        P(("rep", "shard"), None),
        P("shard", None),
        P("shard", None),
        P("shard", None),
        P("shard", None),
        P("shard"),
        P("shard"),
        P("shard"),
        P("shard"),
        P("shard", None),
        P("shard", None),
        P("shard", None),
        P("shard"),
    )
    return jax.shard_map(
        on_device, mesh=mesh, in_specs=in_specs, out_specs=out_specs, check_vma=False
    )
```

profile of v0, /device:TPU:0, one launch (start us, length us, event | category | flops | bytes accessed | tf_op | source)
XLA Modules:
  0.0 711.2 jit_solution(1980135578788501737)
XLA Ops:
  8.8 0.9 constant_dynamic-update-slice_fusion.3
  11.3 1.0 constant_dynamic-update-slice_fusion
  13.2 1.9 constant_dynamic-slice_fusion.1
  15.1 0.9 concatenate.94
  16.1 0.9 concatenate.95
  18.5 11.2 %all_gather.44 = bf16[512,896]{1,0:T(8,128)(2,1)} all-gather(bf16[128,896]{1,0:T(8,128)(2,1)S(1)} %copy-done.7), channel_id=1, replica_groups=mesh['rep'=4,'shard'=8] {'rep'}, dimensions={0}, use_global_device_ids=true | all-gather | bytes 1146880 | tf_op jit(solution)/shard_map/all_gather | solution.py:171
  29.9 55.2 %all-gather.11.cloned.1.call-done = bf16[896,2176]{1,0:T(8,128)(2,1)} async-done(((bf16[112,2176]{1,0:T(8,128)(2,1)}), bf16[896,2176]{1,0:T(8,128)(2,1)}) %all-gather.11.cloned.1.call-update) | async-done | bytes 3899408 | tf_op jit(solution)/shard_map/all_gather | solution.py:154
  85.1 1.0 slice_bitcast_fusion
  87.2 2.1 convolution_add_fusion
  90.7 2.0 multiply_reduce_fusion
  92.8 9.9 %all_gather.40 = bf16[512,896]{1,0:T(8,128)(2,1)} all-gather(bf16[128,896]{1,0:T(8,128)(2,1)S(1)} %multiply_convert_fusion.3), channel_id=1, replica_groups=mesh['rep'=4,'shard'=8] {'rep'}, dimensions={0}, use_global_device_ids=true | all-gather | bytes 1146880 | tf_op jit(solution)/shard_map/all_gather | solution.py:185
  102.7 34.8 %all-gather.13.cloned.1.call-done = bf16[896,1216]{1,0:T(8,128)(2,1)} async-done(((bf16[112,1216]{1,0:T(8,128)(2,1)}), bf16[896,1216]{1,0:T(8,128)(2,1)}) %all-gather.13.cloned.1.call-update) | async-done | bytes 2179088 | tf_op jit(solution)/shard_map/all_gather | solution.py:164
  137.5 4.9 fusion.66
  142.4 47.5 %all-gather.15.cloned.1.call-done = bf16[896,1216]{1,0:T(8,128)(2,1)} async-done(((bf16[112,1216]{1,0:T(8,128)(2,1)}), bf16[896,1216]{1,0:T(8,128)(2,1)}) %all-gather.15.cloned.1.call-update) | async-done | bytes 2179088 | tf_op jit(solution)/shard_map/all_gather | solution.py:167
  189.8 5.0 fusion.67
  194.8 46.3 %all-gather.17.cloned.1.call-done = bf16[1216,896]{1,0:T(8,128)(2,1)} async-done(((bf16[152,896]{1,0:T(8,128)(2,1)}), bf16[1216,896]{1,0:T(8,128)(2,1)}) %all-gather.17.cloned.1.call-update) | async-done | bytes 2179088 | tf_op jit(solution)/shard_map/all_gather | solution.py:168
  241.1 7.0 multiply_convert_fusion
  248.1 1.6 fusion.68
  250.7 2.6 add_convert_fusion
  253.3 4.5 convolution_convert_fusion.5
  257.9 4.5 convolution_convert_fusion.1
  262.5 4.4 convolution_convert_fusion.2
  267.1 4.5 convolution_convert_fusion
  271.7 4.2 reduce-scatter.12.cloned.1.call-done
  275.9 1.1 fusion.27
  277.1 25.3 %reduce-scatter.10.cloned.1.call-done = bf16[128,896]{1,0:T(8,128)(2,1)} async-done(((bf16[512,896]{1,0:T(8,128)(2,1)}), bf16[128,896]{1,0:T(8,128)(2,1)}) %reduce-scatter.10.cloned.1.call-update) | async-done | bytes 229392 | tf_op jit(solution)/shard_map/reduce_scatter | solution.py:204
  302.4 1.9 fusion.24
  304.3 2.0 fusion.17
  308.0 1.4 copy-done.3
  312.7 2.1 pad_maximum_fusion
  314.8 60.8 %reduce-scatter.20.cloned.1.call-done = bf16[112,1216]{1,0:T(8,128)(2,1)} async-done(((bf16[896,1216]{1,0:T(8,128)(2,1)}), bf16[112,1216]{1,0:T(8,128)(2,1)}) %reduce-scatter.20.cloned.1.call-update) | async-done | bytes 272400 | tf_op jit(solution)/shard_map/reduce_scatter | solution.py:202
  375.7 72.2 %reduce-scatter.18.cloned.1.call-done = bf16[112,1216]{1,0:T(8,128)(2,1)} async-done(((bf16[896,1216]{1,0:T(8,128)(2,1)}), bf16[112,1216]{1,0:T(8,128)(2,1)}) %reduce-scatter.18.cloned.1.call-update) | async-done | bytes 272400 | tf_op jit(solution)/shard_map/reduce_scatter | solution.py:201
  448.0 77.8 %reduce-scatter.22.cloned.1.call-done = bf16[152,896]{1,0:T(8,128)(2,1)} async-done(((bf16[1216,896]{1,0:T(8,128)(2,1)}), bf16[152,896]{1,0:T(8,128)(2,1)}) %reduce-scatter.22.cloned.1.call-update) | async-done | bytes 272400
  525.8 86.8 %reduce-scatter.14.cloned.1.call-done = bf16[112,2176]{1,0:T(8,128)(2,1)} async-done(((bf16[896,2176]{1,0:T(8,128)(2,1)}), bf16[112,2176]{1,0:T(8,128)(2,1)}) %reduce-scatter.14.cloned.1.call-update) | async-done | bytes 487440 | tf_op jit(solution)/shard_map/reduce_scatter | solution.py:240
  614.3 1.0 fusion.62
  616.3 1.0 fusion.34
  617.2 14.0 %all-gather.23.cloned.1.call-done = bf16[448,1216]{1,0:T(8,128)(2,1)} async-done(((bf16[112,1216]{1,0:T(8,128)(2,1)}), bf16[448,1216]{1,0:T(8,128)(2,1)}) %all-gather.23.cloned.1.call-update) | async-done | bytes 1089552 | tf_op jit(solution)/shard_map/all_gather | solution.py:256
  631.2 1.6 fusion.59
  633.3 3.9 concatenate.107
  637.2 1.5 convert_element_type.175
  638.7 11.2 %all-gather.21.cloned.1.call-done = bf16[448,1216]{1,0:T(8,128)(2,1)} async-done(((bf16[112,1216]{1,0:T(8,128)(2,1)}), bf16[448,1216]{1,0:T(8,128)(2,1)}) %all-gather.21.cloned.1.call-update) | async-done | bytes 1089552 | tf_op jit(solution)/shard_map/all_gather | solution.py:256
  649.9 1.6 fusion.61
  652.0 3.8 concatenate.106
  655.9 1.5 convert_element_type.173
  657.4 11.1 %all-gather.19.cloned.1.call-done = bf16[608,896]{1,0:T(8,128)(2,1)} async-done(((bf16[152,896]{1,0:T(8,128)(2,1)}), bf16[608,896]{1,0:T(8,128)(2,1)}) %all-gather.19.cloned.1.call-update) | async-done | bytes 1089552 | tf_op jit(solution)/shard_map/all_gather | solution.py:253
  668.4 2.7 convert_element_type.177
  671.2 21.6 %reduce-scatter.16.cloned.1.call-done = bf16[112,640]{1,0:T(8,128)(2,1)} async-done(((bf16[448,640]{1,0:T(8,128)(2,1)}), bf16[112,640]{1,0:T(8,128)(2,1)}) %reduce-scatter.16.cloned.1.call-update) | async-done | bytes 143376 | tf_op jit(solution)/shard_map/reduce_scatter | solution.py:247
  695.9 6.5 all-gather
  (134 shorter events, 23.7 us)
Async XLA Ops:
  7.2 9.9 %copy-start = (bf16[608,896]{1,0:T(8,128)(2,1)S(1)}, bf16[608,896]{1,0:T(8,128)(2,1)}, u32[]{:S(2)}) copy-start(bf16[608,896]{1,0:T(8,128)(2,1)} %param.28) | copy-start | bytes 3268612
  7.2 77.9 %all-gather.11.cloned.1.call-start = ((), (), s32[]{:S(2)}) async-start(), calls=%async_computation.7 | async-start | bytes 4386816 | tf_op jit(solution)/shard_map/all_gather | solution.py:154
  12.3 0.8 copy-start.6
  13.1 124.4 %all-gather.13.cloned.1.call-start = ((), (), s32[]{:S(2)}) async-start(), calls=%async_computation.8 | async-start | bytes 2580480 | tf_op jit(solution)/shard_map/all_gather | solution.py:164
  13.2 4.8 copy-start.10
  13.2 5.1 copy-start.2
  13.2 5.3 copy-start.7
  16.0 173.8 %all-gather.15.cloned.1.call-start = ((), (), s32[]{:S(2)}) async-start(), calls=%async_computation.9 | async-start | bytes 2580480 | tf_op jit(solution)/shard_map/all_gather | solution.py:167
  17.1 224.0 %all-gather.17.cloned.1.call-start = ((), (), s32[]{:S(2)}) async-start(), calls=%async_computation.10 | async-start | bytes 2451456 | tf_op jit(solution)/shard_map/all_gather | solution.py:168
  17.9 258.0 %reduce-scatter.12.cloned.1.call-start = ((), (), s32[]{:S(2)}) async-start(), calls=%async_computation.12 | async-start | bytes 1146880 | tf_op jit(solution)/shard_map/reduce_scatter | solution.py:194
  241.1 7.0 copy-start.8
  248.1 1.6 copy-start.11
  248.1 1.6 copy-start.12
  248.1 2.5 copy-start.9
  253.3 49.1 %reduce-scatter.10.cloned.1.call-start = ((), (), s32[]{:S(2)}) async-start(), calls=%async_computation.11 | async-start | bytes 1146880 | tf_op jit(solution)/shard_map/reduce_scatter | solution.py:204
  257.8 117.8 %reduce-scatter.20.cloned.1.call-start = ((), (), s32[]{:S(2)}) async-start(), calls=%async_computation.16 | async-start | bytes 2580480 | tf_op jit(solution)/shard_map/reduce_scatter | solution.py:202
  262.4 185.5 %reduce-scatter.18.cloned.1.call-start = ((), (), s32[]{:S(2)}) async-start(), calls=%async_computation.15 | async-start | bytes 2580480 | tf_op jit(solution)/shard_map/reduce_scatter | solution.py:201
  266.9 258.9 %reduce-scatter.22.cloned.1.call-start = ((), (), s32[]{:S(2)}) async-start(), calls=%async_computation.20 | async-start | bytes 2451456
  271.6 341.0 %reduce-scatter.14.cloned.1.call-start = ((), (), s32[]{:S(2)}) async-start(), calls=%async_computation.13 | async-start | bytes 4386816 | tf_op jit(solution)/shard_map/reduce_scatter | solution.py:240
  307.3 2.1 copy-start.3
  314.7 316.5 %all-gather.23.cloned.1.call-start = ((), (), s32[]{:S(2)}) async-start(), calls=%async_computation.19 | async-start | bytes 1433600 | tf_op jit(solution)/shard_map/all_gather | solution.py:256
  375.6 274.3 %all-gather.21.cloned.1.call-start = ((), (), s32[]{:S(2)}) async-start(), calls=%async_computation.18 | async-start | bytes 1433600 | tf_op jit(solution)/shard_map/all_gather | solution.py:256
  447.9 220.5 %all-gather.19.cloned.1.call-start = ((), (), s32[]{:S(2)}) async-start(), calls=%async_computation.17 | async-start | bytes 1361920 | tf_op jit(solution)/shard_map/all_gather | solution.py:253
  525.8 167.0 %reduce-scatter.16.cloned.1.call-start = ((), (), s32[]{:S(2)}) async-start(), calls=%async_computation.14 | async-start | bytes 716800 | tf_op jit(solution)/shard_map/reduce_scatter | solution.py:247
  631.2 1.7 copy-start.5
  649.9 1.7 copy-start.4
  695.8 8.8 %copy-start.1 = (bf16[608,896]{1,0:T(8,128)(2,1)S(1)}, bf16[608,896]{1,0:T(8,128)(2,1)}, u32[]{:S(2)}) copy-start(bf16[608,896]{1,0:T(8,128)(2,1)} %param.28) | copy-start | bytes 3268612
Sparse Core Ops, SparseCore 0:
  13.2 71.7 all-gather.10
  87.8 49.6 all-gather.12
  140.3 49.5 all-gather.14
  192.5 48.5 all-gather.16
  253.4 22.4 reduce-scatter.11
  278.3 23.9 reduce-scatter.9
  305.9 69.6 reduce-scatter.19
  379.1 68.7 reduce-scatter.17
  451.9 73.7 reduce-scatter.21
  529.1 83.4 reduce-scatter.13
  614.2 16.9 all-gather.22
  632.6 17.2 all-gather.20
  651.5 16.9 all-gather.18
  670.8 21.9 reduce-scatter.15
where the time goes:
time: 712 us; the launch traced here: 711 us
  waiting for transfers between devices  569 us (80%)
  matrix products  49 us (7%)
  local copies, waits for them, and re-layouts  33.5 us (5%)
  blocking collectives  27.6 us (4%)
  other arithmetic  16.8 us (2%)
  between operations  14.4 us (2%)
    reduce_scatter x1, waiting for transfers between devices, on_device(): owned = lax.psum_scatter(packed_g, 'shard', scatter_dimension=0, tiled=True)  86.8 us
    unnamed x15, waiting for transfers between devices  78 us
    reduce_scatter x1, waiting for transfers between devices, on_device(): lax.psum_scatter(grad_gate, 'shard', scatter_dimension=0, tiled=True)  72.2 us
    reduce_scatter x1, waiting for transfers between devices, on_device(): lax.psum_scatter(grad_up, 'shard', scatter_dimension=0, tiled=True)  60.8 us
    all_gather x1, waiting for transfers between devices, on_device(): packed = lax.all_gather(packed, 'shard', axis=0, tiled=True)  55.2 us
    all_gather x1, waiting for transfers between devices, on_device(): lax.all_gather(share_of(up_weight, rep, shards, reps), 'shard', axis=0, t...  47.5 us
    all_gather x1, waiting for transfers between devices, on_device(): lax.all_gather(lax.dynamic_slice(down_weight, (rep * part, 0), (part, wid...  46.3 us
    all_gather x1, waiting for transfers between devices, on_device(): lax.all_gather(share_of(gate_weight, rep, shards, reps), 'shard', axis=0,...  34.8 us
  transfers between devices with their start and end apart: 14, of which 14 were waited for; matrix products, arithmetic and copies ran while one was open for 10% of the time, Pallas kernels for 0%

commit v1 on v0

--- a/solution.py
+++ b/solution.py
@@ -10,6 +10,12 @@
 theta_base = 1000000.0
 eps_norm = 1e-06
 masked_score = -1000000000.0
+
+
+def joined_along(pieces, dim):
+    lengths = list(pieces.shape[1:])
+    lengths[dim] *= pieces.shape[0]
+    return jnp.moveaxis(pieces, 0, dim).reshape(lengths)
 
 
 def times_transposed(left, weight):
@@ -164,7 +170,20 @@
     gate_mine = lax.all_gather(
         share_of(gate_weight, rep, shards, reps), "shard", axis=0, tiled=True
     )
-    up_mine = lax.all_gather(share_of(up_weight, rep, shards, reps), "shard", axis=0, tiled=True)
+    x = share_of(up_weight, rep, shards, reps)
+    size = lax.axis_size("shard")
+    pairs = [(i_2, (i_2 + 1) % size) for i_2 in range(size)]
+    back = [(b, a) for a, b in pairs]
+    lower, upper_2 = ([], [])
+    for hop in range(size - 1):
+        if hop % 2 == 0:
+            lower.append(lax.ppermute(lower[-1] if lower else x, "shard", pairs))
+        else:
+            upper_2.append(lax.ppermute(upper_2[-1] if upper_2 else x, "shard", back))
+    parts = jnp.stack([*lower[::-1], x, *upper_2])
+    shift = lax.axis_index("shard") - len(lower)
+    parts = parts[(jnp.arange(size) - shift) % size]
+    up_mine = joined_along(parts, 0)
     down_mine = lax.all_gather(
         lax.dynamic_slice(down_weight, (rep * part, 0), (part, width)), "shard", axis=0, tiled=True
     )

time: 712 us -> 687 us (0.965)
  waiting for transfers between devices: 569 us -> 524 us
  starting transfers between devices: 0.79 us -> 19 us
    all_gather x1 -> x0, waiting for transfers between devices: 47.5 us -> none  [on_device(): lax.all_gather(share_of(up_weight, rep, shards, reps), 'shard', axis=0, t...]
    all_gather x1, waiting for transfers between devices: 46.3 us -> 3.75 us  [on_device(): lax.all_gather(lax.dynamic_slice(down_weight, (rep * part, 0), (part, wid...]
    ppermute x0 -> x7, waiting for transfers between devices: none -> 37.4 us  [the longest x4 36 us: on_device(): lower.append(lax.ppermute(lower[-1] if lower else x, 'shard', pairs))]
    ppermute x0 -> x7, starting transfers between devices: none -> 18.3 us  [the longest x3 15.4 us: on_device(): upper_2.append(lax.ppermute(upper_2[-1] if upper_2 else x, 'shard', back))]
    all_gather x1, waiting for transfers between devices: 55.2 us -> 66.2 us  [on_device(): packed = lax.all_gather(packed, 'shard', axis=0, tiled=True)]
    unnamed x15 -> x14, waiting for transfers between devices: 78 us -> 78 us
  transfers between devices with their start and end apart: 14 -> 20, of which waited for: 14 -> 19; matrix products, arithmetic and copies ran while one was open for 10% -> 12% of each run, Pallas kernels for 0% -> 0%
where the time goes in v1:
time: 687 us; the launch traced here: 685 us
  waiting for transfers between devices  524 us (76%)
  matrix products  43.1 us (6%)
  local copies, waits for them, and re-layouts  40 us (6%)
  blocking collectives  25.7 us (4%)
  starting transfers between devices  19 us (3%)
  other arithmetic  18.4 us (3%)
  between operations  14.5 us (2%)
    reduce_scatter x1, waiting for transfers between devices, on_device(): owned = lax.psum_scatter(packed_g, 'shard', scatter_dimension=0, tiled=True)  86.9 us
    unnamed x14, waiting for transfers between devices  78 us
    reduce_scatter x1, waiting for transfers between devices, on_device(): lax.psum_scatter(grad_gate, 'shard', scatter_dimension=0, tiled=True)  72.2 us
    all_gather x1, waiting for transfers between devices, on_device(): packed = lax.all_gather(packed, 'shard', axis=0, tiled=True)  66.2 us
    reduce_scatter x1, waiting for transfers between devices, on_device(): lax.psum_scatter(grad_up, 'shard', scatter_dimension=0, tiled=True)  60.6 us
    ppermute x4, waiting for transfers between devices, on_device(): lower.append(lax.ppermute(lower[-1] if lower else x, 'shard', pairs))  36 us
    all_gather x1, waiting for transfers between devices, on_device(): lax.all_gather(share_of(gate_weight, rep, shards, reps), 'shard', axis=0,...  34.6 us
    reduce_scatter x1, waiting for transfers between devices, on_device(): out_sum = lax.psum_scatter(out_part, 'rep', scatter_dimension=0, tiled=True)  25.3 us
  transfers between devices with their start and end apart: 20, of which 19 were waited for; matrix products, arithmetic and copies ran while one was open for 12% of the time, Pallas kernels for 0%

profile of v1, /device:TPU:0, one launch (start us, length us, event | category | flops | bytes accessed | tf_op | source)
XLA Modules:
  0.0 685.1 jit_solution(8262802140376869910)
XLA Ops:
  15.1 1.8 constant_dynamic-slice_fusion.1
  17.2 6.1 collective-permute-start.4
  24.6 9.8 %all_gather.40 = bf16[512,896]{1,0:T(8,128)(2,1)} all-gather(bf16[128,896]{1,0:T(8,128)(2,1)S(1)} %copy-done.7), channel_id=1, replica_groups=mesh['rep'=4,'shard'=8] {'rep'}, dimensions={0}, use_global_device_ids=true | all-gather | bytes 1146880 | tf_op jit(solution)/shard_map/all_gather | solution.py:190
  34.5 3.9 collective-permute-done
  39.3 10.2 %collective-permute-done.1 = bf16[112,1216]{1,0:T(8,128)(2,1)S(1)} collective-permute-done((bf16[112,1216]{1,0:T(8,128)(2,1)S(1)}, bf16[112,1216]{1,0:T(8,128)(2,1)S(1)}, u32[]{:S(2)}, u32[]{:S(2)}) %collective-permute-start.1) | collective-permute-done | bytes 272416 | tf_op jit(solution)/shard_map/ppermute | solution.py:180
  50.2 4.7 collective-permute-start.5
  54.9 13.4 %collective-permute-done.2 = bf16[112,1216]{1,0:T(8,128)(2,1)S(1)} collective-permute-done((bf16[112,1216]{1,0:T(8,128)(2,1)S(1)}, bf16[112,1216]{1,0:T(8,128)(2,1)S(1)}, u32[]{:S(2)}, u32[]{:S(2)}) %collective-permute-start.2) | collective-permute-done | bytes 272416 | tf_op jit(solution)/shard_map/ppermute | solution.py:180
  68.3 2.5 collective-permute-start.3
  71.4 4.6 collective-permute-start.6
  76.0 8.5 %collective-permute-done.3 = bf16[112,1216]{1,0:T(8,128)(2,1)S(1)} collective-permute-done((bf16[112,1216]{1,0:T(8,128)(2,1)S(1)}, bf16[112,1216]{1,0:T(8,128)(2,1)S(1)}, u32[]{:S(2)}, u32[]{:S(2)}) %collective-permute-start.3) | collective-permute-done | bytes 272416 | tf_op jit(solution)/shard_map/ppermute | solution.py:180
  86.7 2.2 gather_fusion
  88.9 3.8 all-gather.14.cloned.1.call-done
  92.6 4.8 convolution_bitcast_fusion
  97.4 66.2 %all-gather.10.cloned.1.call-done = bf16[896,2176]{1,0:T(8,128)(2,1)} async-done(((bf16[112,2176]{1,0:T(8,128)(2,1)}), bf16[896,2176]{1,0:T(8,128)(2,1)}) %all-gather.10.cloned.1.call-update) | async-done | bytes 3899408 | tf_op jit(solution)/shard_map/all_gather | solution.py:160
  165.7 2.1 convolution_add_fusion
  169.4 2.0 multiply_reduce_fusion
  172.0 9.5 %all_gather.37 = bf16[512,896]{1,0:T(8,128)(2,1)S(1)} all-gather(bf16[128,896]{1,0:T(8,128)(2,1)S(1)} %multiply_convert_fusion.3), channel_id=1, replica_groups=mesh['rep'=4,'shard'=8] {'rep'}, dimensions={0}, use_global_device_ids=true | all-gather | bytes 1146880 | tf_op jit(solution)/shard_map/all_gather | solution.py:204
  181.5 34.6 %all-gather.12.cloned.1.call-done = bf16[896,1216]{1,0:T(8,128)(2,1)} async-done(((bf16[112,1216]{1,0:T(8,128)(2,1)}), bf16[896,1216]{1,0:T(8,128)(2,1)}) %all-gather.12.cloned.1.call-update) | async-done | bytes 2179088 | tf_op jit(solution)/shard_map/all_gather | solution.py:170
  216.1 3.3 fusion.68
  219.4 3.8 multiply_convert_fusion
  223.2 1.6 fusion.69
  224.8 2.6 add_convert_fusion
  227.5 4.5 convolution_convert_fusion.5
  232.0 4.2 convolution_convert_fusion.1
  236.3 4.1 convolution_convert_fusion.2
  241.6 4.2 convolution_convert_fusion
  246.0 4.1 reduce-scatter.12.cloned.1.call-done
  251.2 25.3 %reduce-scatter.10.cloned.1.call-done = bf16[128,896]{1,0:T(8,128)(2,1)} async-done(((bf16[512,896]{1,0:T(8,128)(2,1)}), bf16[128,896]{1,0:T(8,128)(2,1)}) %reduce-scatter.10.cloned.1.call-update) | async-done | bytes 229392 | tf_op jit(solution)/shard_map/reduce_scatter | solution.py:223
  276.5 1.9 fusion.24
  278.5 2.0 fusion.17
  286.9 2.0 pad_maximum_fusion
  289.0 60.6 %reduce-scatter.20.cloned.1.call-done = bf16[112,1216]{1,0:T(8,128)(2,1)} async-done(((bf16[896,1216]{1,0:T(8,128)(2,1)}), bf16[112,1216]{1,0:T(8,128)(2,1)}) %reduce-scatter.20.cloned.1.call-update) | async-done | bytes 272400 | tf_op jit(solution)/shard_map/reduce_scatter | solution.py:221
  349.7 72.2 %reduce-scatter.18.cloned.1.call-done = bf16[112,1216]{1,0:T(8,128)(2,1)} async-done(((bf16[896,1216]{1,0:T(8,128)(2,1)}), bf16[112,1216]{1,0:T(8,128)(2,1)}) %reduce-scatter.18.cloned.1.call-update) | async-done | bytes 272400 | tf_op jit(solution)/shard_map/reduce_scatter | solution.py:220
  421.9 77.8 %reduce-scatter.22.cloned.1.call-done = bf16[152,896]{1,0:T(8,128)(2,1)} async-done(((bf16[1216,896]{1,0:T(8,128)(2,1)}), bf16[152,896]{1,0:T(8,128)(2,1)}) %reduce-scatter.22.cloned.1.call-update) | async-done | bytes 272400
  499.8 86.9 %reduce-scatter.14.cloned.1.call-done = bf16[112,2176]{1,0:T(8,128)(2,1)} async-done(((bf16[896,2176]{1,0:T(8,128)(2,1)}), bf16[112,2176]{1,0:T(8,128)(2,1)}) %reduce-scatter.14.cloned.1.call-update) | async-done | bytes 487440 | tf_op jit(solution)/shard_map/reduce_scatter | solution.py:259
  591.2 13.8 %all-gather.20.cloned.1.call-done = bf16[448,1216]{1,0:T(8,128)(2,1)} async-done(((bf16[112,1216]{1,0:T(8,128)(2,1)}), bf16[448,1216]{1,0:T(8,128)(2,1)}) %all-gather.20.cloned.1.call-update) | async-done | bytes 1089552 | tf_op jit(solution)/shard_map/all_gather | solution.py:275
  605.0 1.5 fusion.61
  606.5 1.9 fusion.60
  608.4 3.9 concatenate.107
  612.3 1.5 convert_element_type.175
  613.8 10.1 %all-gather.18.cloned.1.call-done = bf16[448,1216]{1,0:T(8,128)(2,1)} async-done(((bf16[112,1216]{1,0:T(8,128)(2,1)}), bf16[448,1216]{1,0:T(8,128)(2,1)}) %all-gather.18.cloned.1.call-update) | async-done | bytes 1089552 | tf_op jit(solution)/shard_map/all_gather | solution.py:275
  625.4 1.9 fusion.62
  627.3 3.8 concatenate.106
  631.1 1.5 convert_element_type.173
  632.6 9.6 %all-gather.16.cloned.1.call-done = bf16[608,896]{1,0:T(8,128)(2,1)} async-done(((bf16[152,896]{1,0:T(8,128)(2,1)}), bf16[608,896]{1,0:T(8,128)(2,1)}) %all-gather.16.cloned.1.call-update) | async-done | bytes 1089552 | tf_op jit(solution)/shard_map/all_gather | solution.py:272
  642.3 2.7 convert_element_type.177
  645.0 21.7 %reduce-scatter.16.cloned.1.call-done = bf16[112,640]{1,0:T(8,128)(2,1)} async-done(((bf16[448,640]{1,0:T(8,128)(2,1)}), bf16[112,640]{1,0:T(8,128)(2,1)}) %reduce-scatter.16.cloned.1.call-update) | async-done | bytes 143376 | tf_op jit(solution)/shard_map/reduce_scatter | solution.py:266
  669.8 6.5 all-gather
  (170 shorter events, 38.7 us)
Async XLA Ops:
  7.2 1.2 copy-start
  7.2 85.4 %all-gather.14.cloned.1.call-start = ((), (), s32[]{:S(2)}) async-start(), calls=%async_computation.9 | async-start | bytes 2451456 | tf_op jit(solution)/shard_map/all_gather | solution.py:187
  9.2 154.4 %all-gather.10.cloned.1.call-start = ((), (), s32[]{:S(2)}) async-start(), calls=%async_computation.7 | async-start | bytes 4386816 | tf_op jit(solution)/shard_map/all_gather | solution.py:160
  13.2 11.1 %copy-start.16 = (s32[1,8]{1,0:T(1,128)S(1)}, s32[1,8]{1,0:T(1,128)}, u32[]{:S(2)}) copy-start(s32[1,8]{1,0:T(1,128)} %param.17) | copy-start | bytes 100
  13.2 11.3 %copy-start.2 = (bf16[128,896]{1,0:T(8,128)(2,1)S(1)}, bf16[128,896]{1,0:T(8,128)(2,1)}, u32[]{:S(2)}) copy-start(bf16[128,896]{1,0:T(8,128)(2,1)} %param.15) | copy-start | bytes 688132
  14.2 10.4 %copy-start.7 = (bf16[128,896]{1,0:T(8,128)(2,1)S(1)}, bf16[128,896]{1,0:T(8,128)(2,1)}, u32[]{:S(2)}) copy-start(bf16[128,896]{1,0:T(8,128)(2,1)} %param.16) | copy-start | bytes 688132
  14.3 0.8 copy-start.5
  15.1 201.0 %all-gather.12.cloned.1.call-start = ((), (), s32[]{:S(2)}) async-start(), calls=%async_computation.8 | async-start | bytes 2580480 | tf_op jit(solution)/shard_map/all_gather | solution.py:170
  17.2 33.0 %collective-permute-start.4 = (bf16[112,1216]{1,0:T(8,128)(2,1)S(1)}, bf16[112,1216]{1,0:T(8,128)(2,1)S(1)}, u32[]{:S(2)}, u32[]{:S(2)}) collective-permute-start(bf16[112,1216]{1,0:T(8,128)(2,1)S(1)} %concatenate.95), channel_id=1, source_target_pairs={{1,0},{2,1},{3,2},{4,3},{5,4},{6,5},{7,6},{0,7},{9,8},{10,9},{11,1... | collective-permute-start | bytes 817160 | tf_op jit(solution)/shard_map/ppermute | solution.py:182
  23.3 15.1 %collective-permute-start = (bf16[112,1216]{1,0:T(8,128)(2,1)S(1)}, bf16[112,1216]{1,0:T(8,128)(2,1)S(1)}, u32[]{:S(2)}, u32[]{:S(2)}) collective-permute-start(bf16[112,1216]{1,0:T(8,128)(2,1)S(1)} %concatenate.95), channel_id=1, source_target_pairs={{0,1},{1,2},{2,3},{3,4},{4,5},{5,6},{6,7},{7,0},{8,9},{9,10},{10,1... | collective-permute-start | bytes 817160 | tf_op jit(solution)/shard_map/ppermute | solution.py:180
  24.2 225.9 %reduce-scatter.12.cloned.1.call-start = ((), (), s32[]{:S(2)}) async-start(), calls=%async_computation.11 | async-start | bytes 1146880 | tf_op jit(solution)/shard_map/reduce_scatter | solution.py:213
  38.4 32.4 %copy-start.9 = (bf16[112,1216]{1,0:T(8,128)(2,1)}, bf16[112,1216]{1,0:T(8,128)(2,1)S(1)}, u32[]{:S(2)}) copy-start(bf16[112,1216]{1,0:T(8,128)(2,1)S(1)} %collective-permute-done) | copy-start | bytes 817156
  38.4 11.1 %collective-permute-start.1 = (bf16[112,1216]{1,0:T(8,128)(2,1)S(1)}, bf16[112,1216]{1,0:T(8,128)(2,1)S(1)}, u32[]{:S(2)}, u32[]{:S(2)}) collective-permute-start(bf16[112,1216]{1,0:T(8,128)(2,1)S(1)} %collective-permute-done), channel_id=1, source_target_pairs={{0,1},{1,2},{2,3},{3,4},{4,5},{5,6},{6,7},{7,0},{8,9},{9,10},{10,1... | collective-permute-start | bytes 817160 | tf_op jit(solution)/shard_map/ppermute | solution.py:180
  49.5 18.8 %collective-permute-start.2 = (bf16[112,1216]{1,0:T(8,128)(2,1)S(1)}, bf16[112,1216]{1,0:T(8,128)(2,1)S(1)}, u32[]{:S(2)}, u32[]{:S(2)}) collective-permute-start(bf16[112,1216]{1,0:T(8,128)(2,1)S(1)} %collective-permute-done.1), channel_id=1, source_target_pairs={{0,1},{1,2},{2,3},{3,4},{4,5},{5,6},{6,7},{7,0},{8,9},{9,10},{10,1... | collective-permute-start | bytes 817160 | tf_op jit(solution)/shard_map/ppermute | solution.py:180
  50.2 21.2 %collective-permute-start.5 = (bf16[112,1216]{1,0:T(8,128)(2,1)S(1)}, bf16[112,1216]{1,0:T(8,128)(2,1)S(1)}, u32[]{:S(2)}, u32[]{:S(2)}) collective-permute-start(bf16[112,1216]{1,0:T(8,128)(2,1)S(1)} %collective-permute-done.4), channel_id=1, source_target_pairs={{1,0},{2,1},{3,2},{4,3},{5,4},{6,5},{7,6},{0,7},{9,8},{10,9},{11,1... | collective-permute-start | bytes 817160 | tf_op jit(solution)/shard_map/ppermute | solution.py:182
  68.3 16.2 %collective-permute-start.3 = (bf16[112,1216]{1,0:T(8,128)(2,1)S(1)}, bf16[112,1216]{1,0:T(8,128)(2,1)S(1)}, u32[]{:S(2)}, u32[]{:S(2)}) collective-permute-start(bf16[112,1216]{1,0:T(8,128)(2,1)S(1)} %collective-permute-done.2), channel_id=1, source_target_pairs={{0,1},{1,2},{2,3},{3,4},{4,5},{5,6},{6,7},{7,0},{8,9},{9,10},{10,1... | collective-permute-start | bytes 817160 | tf_op jit(solution)/shard_map/ppermute | solution.py:180
  71.4 15.3 %collective-permute-start.6 = (bf16[112,1216]{1,0:T(8,128)(2,1)S(1)}, bf16[112,1216]{1,0:T(8,128)(2,1)S(1)}, u32[]{:S(2)}, u32[]{:S(2)}) collective-permute-start(bf16[112,1216]{1,0:T(8,128)(2,1)S(1)} %collective-permute-done.5), channel_id=1, source_target_pairs={{1,0},{2,1},{3,2},{4,3},{5,4},{6,5},{7,6},{0,7},{9,8},{10,9},{11,1... | collective-permute-start | bytes 817160 | tf_op jit(solution)/shard_map/ppermute | solution.py:182
  167.9 0.7 copy-start.12
  168.4 2.9 copy-start.10
  216.1 3.3 copy-start.4
  216.1 3.3 copy-start.17
  219.4 3.8 copy-start.15
  223.2 1.6 copy-start.18
  223.2 1.6 copy-start.19
  227.4 49.1 %reduce-scatter.10.cloned.1.call-start = ((), (), s32[]{:S(2)}) async-start(), calls=%async_computation.10 | async-start | bytes 1146880 | tf_op jit(solution)/shard_map/reduce_scatter | solution.py:223
  232.0 117.6 %reduce-scatter.20.cloned.1.call-start = ((), (), s32[]{:S(2)}) async-start(), calls=%async_computation.15 | async-start | bytes 2580480 | tf_op jit(solution)/shard_map/reduce_scatter | solution.py:221
  236.2 185.6 %reduce-scatter.18.cloned.1.call-start = ((), (), s32[]{:S(2)}) async-start(), calls=%async_computation.14 | async-start | bytes 2580480 | tf_op jit(solution)/shard_map/reduce_scatter | solution.py:220
  240.4 1.2 copy-start.6
  240.4 259.3 %reduce-scatter.22.cloned.1.call-start = ((), (), s32[]{:S(2)}) async-start(), calls=%async_computation.19 | async-start | bytes 2451456
  245.7 30.8 %copy-start.8 = (bf16[128,896]{1,0:T(8,128)(2,1)S(1)}, bf16[128,896]{1,0:T(8,128)(2,1)}, u32[]{:S(2)}) copy-start(bf16[128,896]{1,0:T(8,128)(2,1)} %param.16) | copy-start | bytes 688132
  245.7 30.8 %copy-start.14 = (f32[128]{0:T(128)S(1)}, f32[128]{0:T(128)}, u32[]{:S(2)}) copy-start(f32[128]{0:T(128)} %get-tuple-element.138) | copy-start | bytes 1540
  245.7 340.9 %reduce-scatter.14.cloned.1.call-start = ((), (), s32[]{:S(2)}) async-start(), calls=%async_computation.12 | async-start | bytes 4386816 | tf_op jit(solution)/shard_map/reduce_scatter | solution.py:259
  280.5 1.0 copy-start.11
  281.5 2.1 copy-start.3
  288.9 301.3 %copy-start.13 = (f32[128]{0:T(128)S(1)}, f32[128]{0:T(128)}, u32[]{:S(2)}) copy-start(f32[128]{0:T(128)} %get-tuple-element.136) | copy-start | bytes 1540
  288.9 316.1 %all-gather.20.cloned.1.call-start = ((), (), s32[]{:S(2)}) async-start(), calls=%async_computation.18 | async-start | bytes 1433600 | tf_op jit(solution)/shard_map/all_gather | solution.py:275
  349.6 274.3 %all-gather.18.cloned.1.call-start = ((), (), s32[]{:S(2)}) async-start(), calls=%async_computation.17 | async-start | bytes 1433600 | tf_op jit(solution)/shard_map/all_gather | solution.py:275
  421.9 220.4 %all-gather.16.cloned.1.call-start = ((), (), s32[]{:S(2)}) async-start(), calls=%async_computation.16 | async-start | bytes 1361920 | tf_op jit(solution)/shard_map/all_gather | solution.py:272
  499.7 167.0 %reduce-scatter.16.cloned.1.call-start = ((), (), s32[]{:S(2)}) async-start(), calls=%async_computation.13 | async-start | bytes 716800 | tf_op jit(solution)/shard_map/reduce_scatter | solution.py:266
  669.8 8.8 %copy-start.1 = (bf16[608,896]{1,0:T(8,128)(2,1)S(1)}, bf16[608,896]{1,0:T(8,128)(2,1)}, u32[]{:S(2)}) copy-start(bf16[608,896]{1,0:T(8,128)(2,1)} %param.28) | copy-start | bytes 3268612
Sparse Core Ops, SparseCore 0:
  10.8 81.7 all-gather.13
  95.4 68.1 all-gather.9
  166.4 49.6 all-gather.11
  227.6 22.4 reduce-scatter.11
  252.5 23.9 reduce-scatter.9
  279.9 69.6 reduce-scatter.19
  353.1 68.7 reduce-scatter.17
  425.9 73.7 reduce-scatter.21
  503.3 83.3 reduce-scatter.13
  588.1 16.9 all-gather.19
  606.6 17.2 all-gather.17
  625.3 16.9 all-gather.15
  644.8 21.9 reduce-scatter.15
